TPU v7x, 32 devices: a whole 2x2x4 slice. The times are simulated.
32 devices in a mesh: pair: 4 (over z), virt: 8 (over y, x, core).
Axes of the slice: x: 2, y: 2, z: 4, core: 2. Of those that a mesh axis runs over, the one named last changes fastest.
Arguments:
- amplitudes: bfloat16 [4, 8, 2048, 2048], P('pair', None, 'virt'), may hold values from -6 to 6
- factor: bfloat16 [8192, 1024], P('virt'), may hold values from -0.125 to 0.125
- home: int32 [128], replicated, may hold values from 0 to 127, as said below
- domains: int32 [4, 32], P('pair'), may hold values from 0 to 127, as said below
- coupling: bfloat16 [1024, 1024], P('virt'), may hold values from -6 to 6
- hole_weight: bfloat16 [4, 3, 1024], P('pair', None, 'virt'), may hold values from -3 to 3
- virt_energy: float32 [8192], replicated, may hold values from 0.1 to 1
- occ_i: float32 [8], replicated, may hold values from -0.6 to -0.1
- occ_j: float32 [4], P('pair'), may hold values from -0.6 to -0.1
Outputs:
- residual: float32 [4, 8, 2048, 2048], P('pair', None, 'virt')
Inputs may be any that keep to these rules, and one draw needn't show every extreme that they name: `home`: a permutation of the virtual tiles; device k of virt stores the factor rows of slots k * 16 to (k + 1) * 16 - 1. `domains`: each row lists 32 distinct virtual tiles; at most 4 of a row's tiles are stored on any one device of virt, and in every row some device stores exactly 4 of them.
All inputs are finite; a program needn't handle non-finite values.
Results may differ from a plain program's by a relative error of at most 0.0033.
Values may be sent and summed in bfloat16 or wider, within the bound.
No kernel may reach another device: no remote copies, remote signals or barrier semaphores. Data moves between devices by JAX's collectives and lax.ppermute only.
A program may use at most 128 MiB of HBM per device.

v0:
```python
import jax
import jax.numpy as jnp
from jax import lax
from jax.sharding import PartitionSpec as P

TILE = 64
CAP = 4


def with_halo(array, sides, width):
    for axis, dim in sides:
        peers, length = (lax.axis_size(axis), array.shape[dim])
        up = [(i, (i + 1) % peers) for i in range(peers - 1)]
        down = [(j, i) for i, j in up]
        last = lax.slice_in_dim(array, length - width, length, axis=dim)
        first = lax.slice_in_dim(array, 0, width, axis=dim)
        before = lax.ppermute(last, axis, up)
        after = lax.ppermute(first, axis, down)
        array = jnp.concatenate([before, array, after], axis=dim)
    return array


def on_device(amplitudes, factor, home, domains, coupling, hole_weight, virt_energy, occ_i, occ_j):
    factor_cols = factor.shape[1]
    per_device = factor.shape[0] // TILE
    tile_total = home.shape[0]
    domain_entry_row = domains[0]
    slot_of = jnp.sum(
        jnp.where(
            home[None, :] == domain_entry_row[:, None],
            jnp.arange(tile_total, dtype=jnp.int32)[None, :],
            0,
        ),
        axis=1,
    )
    holder = slot_of // per_device
    offset = slot_of % per_device
    domain_len = domain_entry_row.shape[0]
    earlier = jnp.arange(domain_len)[None, :] < jnp.arange(domain_len)[:, None]
    same_holder = holder[None, :] == holder[:, None]
    position = jnp.sum((earlier & same_holder).astype(jnp.int32), axis=1)
    locally_owned = holder == lax.axis_index("virt")
    chosen = locally_owned[None, :] & (
        position[None, :] == jnp.arange(CAP, dtype=jnp.int32)[:, None]
    )
    local_slot = jnp.sum(jnp.where(chosen, offset[None, :], 0), axis=1)
    filled = jnp.any(chosen, axis=1)
    own_tiles = factor.reshape(per_device, TILE, factor_cols)
    outgoing = jnp.where(filled[:, None, None], own_tiles[local_slot], jnp.zeros((), factor.dtype))
    arrived = lax.all_gather(outgoing, "virt", axis=0, tiled=True)
    domain_coefficient = arrived[holder * CAP + position].reshape(-1, factor_cols)
    cluster_amplitude = amplitudes[0]
    half = jnp.einsum(
        "hjm,mf->hfj", cluster_amplitude, domain_coefficient, preferred_element_type=jnp.float32
    ).astype(jnp.bfloat16)
    projected = jnp.einsum(
        "iqd,dp->iqp",
        lax.all_to_all(half, "virt", split_axis=1, concat_axis=2, tiled=True),
        domain_coefficient,
        preferred_element_type=jnp.float32,
    ).astype(jnp.bfloat16)
    neighbours = with_halo(projected[None], (("pair", 0),), 1)
    weights = hole_weight[0].astype(jnp.float32)
    hole = (
        weights[0][None, :, None] * neighbours[0].astype(jnp.float32)
        + weights[1][None, :, None] * neighbours[1].astype(jnp.float32)
        + weights[2][None, :, None] * neighbours[2].astype(jnp.float32)
    )
    dressed = (coupling.astype(jnp.float32)[None] * projected.astype(jnp.float32) + hole).astype(
        jnp.bfloat16
    )
    back = jnp.einsum(
        "iqp,ap->iqa", dressed, domain_coefficient, preferred_element_type=jnp.float32
    ).astype(jnp.bfloat16)
    ladder = jnp.einsum(
        "iqa,bq->iab",
        lax.all_to_all(back, "virt", split_axis=2, concat_axis=1, tiled=True),
        domain_coefficient,
        preferred_element_type=jnp.float32,
    )
    rows_here = cluster_amplitude.shape[1]
    domain_width = cluster_amplitude.shape[2]
    spots = jnp.arange(domain_width, dtype=jnp.int32)
    orbitals = domain_entry_row[spots // TILE] * TILE + spots % TILE
    col_energy = virt_energy[orbitals]
    row_energy = lax.dynamic_slice_in_dim(col_energy, lax.axis_index("virt") * rows_here, rows_here)
    shift = row_energy[None, :, None] + col_energy[None, None, :] - occ_i[:, None, None] - occ_j[0]
    return (ladder + shift * cluster_amplitude.astype(jnp.float32))[None]


def solution(mesh):
    placed = (
        P("pair", None, "virt", None),
        P("virt", None),
        P(),
        P("pair", None),
        P("virt", None),
        P("pair", None, "virt"),
        P(),
        P(),
        P("pair"),
    )
    return jax.shard_map(
        on_device,
        mesh=mesh,
        in_specs=placed,
        out_specs=P("pair", None, "virt", None),
        check_vma=False,
    )
```

profile of v0, /device:TPU:0, one launch (start us, length us, event | category | flops | bytes accessed | tf_op | source)
XLA Modules:
  0.0 298.6 jit_solution(13571353873547823776)
XLA Ops:
  6.5 1.0 select_reduce_fusion
  9.7 39.4 %all-gather.2.cloned.1.call-done = bf16[32,64,1024]{2,1,0:T(8,128)(2,1)} async-done(((bf16[4,64,1024]{2,1,0:T(8,128)(2,1)}), bf16[32,64,1024]{2,1,0:T(8,128)(2,1)}) %all-gather.2.cloned.1.call-update) | async-done | bytes 4194320 | tf_op jit(solution)/shard_map/all_gather | solution.py:50
  49.1 4.9 %gather_fusion.1 = bf16[32,64,1024]{2,1,0:T(8,128)(2,1)} fusion(bf16[32,64,1024]{2,1,0:T(8,128)(2,1)} %all-gather.2.cloned.1.call-done, s32[1024]{0:T(1024)S(1)} %pad_clamp_fusion), kind=kCustom, calls=%fused_computation.1 | custom fusion | bytes 8388736 | tf_op jit(solution)/shard_map/gather | solution.py:51
  54.1 12.6 %convert_bitcast_fusion = bf16[8,1024,256]{2,1,0:T(8,128)(2,1)S(1)} fusion(bf16[2048,1024,1]{1,0,2:T(8,128)(2,1)} %bitcast.116, bf16[1,8,256,2048]{3,2,1,0:T(8,128)(2,1)} %param.9), kind=kOutput, calls=%fused_computation.16 | convolution fusion | flops 8592031744 | bytes 16777216 | tf_op jit(solution)/shard_map/hjm,mf->hfj/dot_general | solution.py:53
  66.7 2.4 copy.22
  69.1 51.6 %all_to_all.36 = bf16[8,1024,256]{2,0,1:T(8,128)(2,1)S(1)} all-to-all(bf16[8,1024,256]{2,0,1:T(8,128)(2,1)S(1)} %copy.22), channel_id=1, replica_groups=mesh['pair'=4,'virt'=8] {'virt'}, dimensions={1} | all-to-all | bytes 8388608 | tf_op jit(solution)/shard_map/all_to_all | solution.py:58
  120.7 4.4 %copy.31 = bf16[8,8,128,256]{3,1,2,0:T(8,128)(2,1)} copy(bf16[8,8,128,256]{3,0,2,1:T(8,128)(2,1)S(1)} %bitcast.113) | data formatting | bytes 8388608 | tf_op jit(solution)/shard_map/all_to_all | solution.py:58
  125.1 7.4 %all_to_all.29 = bf16[8,128,2048]{2,1,0:T(8,128)(2,1)} reshape(bf16[8,128,8,256]{3,2,1,0:T(8,128)(2,1)} %bitcast.114) | data formatting | bytes 8388608 | tf_op jit(solution)/shard_map/all_to_all | solution.py:58
  132.5 8.1 %convolution_convert_fusion.1 = bf16[8,128,1024]{2,1,0:T(8,128)(2,1)S(1)} fusion(bf16[8,128,2048]{2,1,0:T(8,128)(2,1)} %all_to_all.29, bf16[2048,1024,1]{1,0,2:T(8,128)(2,1)} %bitcast.117), kind=kOutput, calls=%fused_computation.24 | convolution fusion | flops 4296015872 | bytes 10485760 | tf_op jit(solution)/shard_map/iqd,dp->iqp/dot_general | solution.py:56
  140.6 1.3 collective-permute-start.1
  141.9 4.7 %collective-permute-start = (bf16[1,8,128,1024]{3,2,1,0:T(8,128)(2,1)S(1)}, bf16[1,8,128,1024]{3,2,1,0:T(8,128)(2,1)S(1)}, u32[]{:S(2)}, u32[]{:S(2)}) collective-permute-start(bf16[1,8,128,1024]{3,2,1,0:T(8,128)(2,1)S(1)} %bitcast.125), channel_id=1, source_target_pairs={{0,8},{8,16},{16,24},{1,9},{9,17},{17,25},{2,10},{10,18},{18,26},{... | collective-permute-start | bytes 6291464 | tf_op jit(solution)/shard_map/ppermute | solution.py:17
  146.7 42.6 %collective-permute-done.1 = bf16[1,8,128,1024]{3,2,1,0:T(8,128)(2,1)S(1)} collective-permute-done((bf16[1,8,128,1024]{3,2,1,0:T(8,128)(2,1)S(1)}, bf16[1,8,128,1024]{3,2,1,0:T(8,128)(2,1)S(1)}, u32[]{:S(2)}, u32[]{:S(2)}) %collective-permute-start.1) | collective-permute-done | bytes 2097184 | tf_op jit(solution)/shard_map/ppermute | solution.py:18
  189.3 1.2 collective-permute-done
  190.5 7.3 %convolution_convert_fusion = bf16[8,128,2048]{2,1,0:T(8,128)(2,1)} fusion(bf16[2048,1024,1]{1,0,2:T(8,128)(2,1)S(1)} %bitcast.119, bf16[8,128,1024]{2,1,0:T(8,128)(2,1)S(1)} %convolution_convert_fusion.1, bf16[1,8,128,1024]{3,2,1,0:T(8,128)(2,1)S(1)} %collective-permute-done.1, bf16[1,8,128,1024]{3,2,1,0:T(8,128)(2,1)S(1)} %collective-permute-done, ...), kind=kOutput, calls=%fused_computation.17 | convolution fusion | flops 4308598784 | bytes 15205888 | tf_op jit(solution)/shard_map/iqp,ap->iqa/dot_general | solution.py:72
  197.7 6.7 %copy.24 = bf16[8,128,2048]{1,0,2:T(8,128)(2,1)} copy(bf16[8,128,2048]{2,1,0:T(8,128)(2,1)} %convolution_convert_fusion) | data formatting | bytes 8388608 | tf_op jit(solution)/shard_map/convert_element_type | solution.py:74
  204.4 4.7 %all-to-all-start.1 = ((bf16[8,128,2048]{1,0,2:T(8,128)(2,1)}), bf16[8,128,2048]{1,0,2:T(8,128)(2,1)}, u32[]{:S(2)}, u32[]{:S(2)}) async-start(bf16[8,128,2048]{1,0,2:T(8,128)(2,1)} %copy.24), calls=%async_computation.1 | async-start | bytes 8388608 | tf_op jit(solution)/shard_map/all_to_all | solution.py:77
  212.6 4.3 %compare_select_fusion.2 = s32[2048,1]{0,1:T(1,128)S(1)} fusion(s32[]{:T(128)} %bitcast.47, s32[]{:T(128)} %bitcast.48, s32[]{:T(128)} %bitcast.49, s32[]{:T(128)} %bitcast.50, s32[]{:T(128)} %bitcast.51, s32[]{:T(128)} %bitcast.53, s32[]{:T(128)} %bitcast.52), kind=kLoop, calls=%fused_computation.54 | loop fusion | flops 47104 | bytes 8220 | tf_op jit(solution)/shard_map/gather | solution.py:84
  216.8 15.7 %select_multiply_fusion = s32[2048]{0:T(1024)S(1)} fusion(pred[2048]{0:T(1024)(128)(4,1)S(1)} %compare_reduce_fusion, pred[2048]{0:T(1024)(128)(4,1)S(1)} %compare_reduce_fusion.1, pred[2048]{0:T(1024)(128)(4,1)S(1)} %compare_reduce_fusion.2, pred[2048]{0:T(1024)(128)(4,1)S(1)} %compare_reduce_fusion.3, pred[2048]{0:T(1024)(128)(4,1)S(1)} %compare_reduce_fusion.4, ...), kind=kLoop, calls=%fused_computation.70 | loop fusion | flops 53248 | bytes 67684 | tf_op jit(solution)/shard_map/mul | solution.py:84
  232.6 11.8 %gather_fusion.2 = f32[2048]{0:T(1024)S(1)} fusion(f32[8192]{0:T(1024)S(1)} %copy-done.2, s32[2048]{0:T(1024)S(1)} %broadcast_clamp_fusion), kind=kCustom, calls=%fused_computation.2 | custom fusion | bytes 24576 | tf_op jit(solution)/shard_map/gather | solution.py:85
  244.4 1.6 broadcast_add_fusion
  246.0 12.2 %all-to-all-done.1 = bf16[8,128,2048]{1,0,2:T(8,128)(2,1)} async-done(((bf16[8,128,2048]{1,0,2:T(8,128)(2,1)}), bf16[8,128,2048]{1,0,2:T(8,128)(2,1)}, u32[]{:S(2)}, u32[]{:S(2)}) %all-to-all-start.1) | async-done | bytes 4194336 | tf_op jit(solution)/shard_map/all_to_all | solution.py:77
  258.2 6.9 %copy.30 = bf16[8,128,8,256]{1,2,3,0:T(8,128)(2,1)} copy(bf16[8,128,8,256]{1,0,3,2:T(8,128)(2,1)} %bitcast.20) | data formatting | bytes 8388608 | tf_op jit(solution)/shard_map/all_to_all | solution.py:77
  265.1 7.3 %all_to_all.33 = bf16[8,1024,256]{1,2,0:T(8,128)(2,1)} reshape(bf16[8,8,128,256]{2,1,3,0:T(8,128)(2,1)} %bitcast.115) | data formatting | bytes 8388608 | tf_op jit(solution)/shard_map/all_to_all | solution.py:77
  272.4 19.3 %add_bitcast_fusion = f32[1,8,256,2048]{3,2,1,0:T(8,128)} fusion(bf16[1,8,256,2048]{3,2,1,0:T(8,128)(2,1)} %param.9, f32[]{:T(128)} %bitcast.111, f32[8]{0:T(128)S(1)} %copy-done.7, f32[256,2048]{1,0:T(8,128)} %broadcast_add_fusion, bf16[8,1024,256]{1,2,0:T(8,128)(2,1)} %all_to_all.33, bf16[2048,1024,1]{1,0,2:T(8,128)(2,1)} %bitcast.118), kind=kOutput, calls=%fused_computation.3 | convolution fusion | flops 8610906112 | bytes 35651620 | tf_op jit(solution)/shard_map/iqa,bq->iab/dot_general | solution.py:75
  (62 shorter events, 5.1 us)
Async XLA Ops:
  6.5 1.6 copy-start
  6.5 42.6 %all-gather.2.cloned.1.call-start = ((), (), s32[]{:S(2)}) async-start(), calls=%async_computation.2 | async-start | bytes 4718592 | tf_op jit(solution)/shard_map/all_gather | solution.py:50
  132.5 14.1 %copy-start.6 = (bf16[1,3,128]{2,1,0:T(4,128)(2,1)S(1)}, bf16[1,3,128]{2,1,0:T(4,128)(2,1)}, u32[]{:S(2)}) copy-start(bf16[1,3,128]{2,1,0:T(4,128)(2,1)} %param.14) | copy-start | bytes 2308
  132.5 14.1 %copy-start.5 = (bf16[128,1024]{1,0:T(8,128)(2,1)S(1)}, bf16[128,1024]{1,0:T(8,128)(2,1)}, u32[]{:S(2)}) copy-start(bf16[128,1024]{1,0:T(8,128)(2,1)} %param.13) | copy-start | bytes 786436
  132.5 58.0 %copy-start.3 = (bf16[32,64,1024]{2,1,0:T(8,128)(2,1)S(1)}, bf16[32,64,1024]{2,1,0:T(8,128)(2,1)}, u32[]{:S(2)}) copy-start(bf16[32,64,1024]{2,1,0:T(8,128)(2,1)} %gather_fusion.1) | copy-start | bytes 12582916
  140.6 48.7 %collective-permute-start.1 = (bf16[1,8,128,1024]{3,2,1,0:T(8,128)(2,1)S(1)}, bf16[1,8,128,1024]{3,2,1,0:T(8,128)(2,1)S(1)}, u32[]{:S(2)}, u32[]{:S(2)}) collective-permute-start(bf16[1,8,128,1024]{3,2,1,0:T(8,128)(2,1)S(1)} %bitcast.124), channel_id=1, source_target_pairs={{8,0},{16,8},{24,16},{9,1},{17,9},{25,17},{10,2},{18,10},{26,18},{... | collective-permute-start | bytes 6291464 | tf_op jit(solution)/shard_map/ppermute | solution.py:18
  141.9 48.6 %collective-permute-start = (bf16[1,8,128,1024]{3,2,1,0:T(8,128)(2,1)S(1)}, bf16[1,8,128,1024]{3,2,1,0:T(8,128)(2,1)S(1)}, u32[]{:S(2)}, u32[]{:S(2)}) collective-permute-start(bf16[1,8,128,1024]{3,2,1,0:T(8,128)(2,1)S(1)} %bitcast.125), channel_id=1, source_target_pairs={{0,8},{8,16},{16,24},{1,9},{9,17},{17,25},{2,10},{10,18},{18,26},{... | collective-permute-start | bytes 6291464 | tf_op jit(solution)/shard_map/ppermute | solution.py:17
  204.4 6.7 %copy-start.4 = (s32[1,32]{1,0:T(1,128)S(1)}, s32[1,32]{1,0:T(1,128)}, u32[]{:S(2)}) copy-start(s32[1,32]{1,0:T(1,128)} %param.12) | copy-start | bytes 388
  204.4 28.1 %copy-start.2 = (f32[8192]{0:T(1024)S(1)}, f32[8192]{0:T(1024)}, u32[]{:S(2)}) copy-start(f32[8192]{0:T(1024)} %param.15) | copy-start | bytes 98308
  204.4 53.8 %all-to-all-start.1 = ((bf16[8,128,2048]{1,0,2:T(8,128)(2,1)}), bf16[8,128,2048]{1,0,2:T(8,128)(2,1)}, u32[]{:S(2)}, u32[]{:S(2)}) async-start(bf16[8,128,2048]{1,0,2:T(8,128)(2,1)} %copy.24), calls=%async_computation.1 | async-start | bytes 8388608 | tf_op jit(solution)/shard_map/all_to_all | solution.py:77
  265.1 7.3 %copy-start.7 = (f32[8]{0:T(128)S(1)}, f32[8]{0:T(128)}, u32[]{:S(2)}) copy-start(f32[8]{0:T(128)} %param.16) | copy-start | bytes 100
  272.4 19.3 %copy-start.1 = (bf16[1024,1024]{1,0:T(8,128)(2,1)S(1)}, bf16[1024,1024]{1,0:T(8,128)(2,1)}, u32[]{:S(2)}) copy-start(bf16[1024,1024]{1,0:T(8,128)(2,1)} %param.10) | copy-start | bytes 6291460
Sparse Core Ops, SparseCore 0:
  9.8 39.2 all-gather.1
where the time goes:
time: 300 us; the launch traced here: 299 us
  waiting for transfers between devices  95.5 us (32%)
  local copies, waits for them, and re-layouts  54.1 us (18%)
  blocking collectives  51.6 us (17%)
  matrix products  47.2 us (16%)
  other arithmetic  25.3 us (8%)
  between operations  14.2 us (5%)
  starting transfers between devices  10.7 us (4%)
    all_to_all x1, blocking collectives, on_device(): lax.all_to_all(half, 'virt', split_axis=1, concat_axis=2, tiled=True)  51.6 us
    ppermute x1, waiting for transfers between devices, with_halo(): after = lax.ppermute(first, axis, down)  42.6 us
    all_gather x1, waiting for transfers between devices, on_device(): arrived = lax.all_gather(outgoing, 'virt', axis=0, tiled=True)  39.4 us
    dot_general x1, matrix products, on_device(): jnp.einsum('iqa,bq->iab', lax.all_to_all(back, 'virt', split_axis=2, conc...  19.3 us
    mul x1, other arithmetic, on_device(): orbitals = domain_entry_row[spots // TILE] * TILE + spots % TILE  15.7 us
    all_to_all x2, local copies, waits for them, and re-layouts, on_device(): lax.all_to_all(back, 'virt', split_axis=2, concat_axis=1, tiled=True)  14.2 us
    dot_general x1, matrix products, on_device(): jnp.einsum('hjm,mf->hfj', cluster_amplitude, domain_coefficient, preferre...  12.6 us
    all_to_all x1, waiting for transfers between devices, on_device(): lax.all_to_all(back, 'virt', split_axis=2, concat_axis=1, tiled=True)  12.2 us
  transfers between devices with their start and end apart: 4, of which 4 were waited for; matrix products, arithmetic and copies ran while one was open for 12% of the time, Pallas kernels for 0%

commit v1 on v0

--- a/solution.py
+++ b/solution.py
@@ -21,6 +21,19 @@
 
 
 def on_device(amplitudes, factor, home, domains, coupling, hole_weight, virt_energy, occ_i, occ_j):
+
+    def points_obtain(body, axis_id):
+        work_now = jnp.concatenate(
+            lax.all_to_all(
+                jnp.stack(jnp.split(body, lax.axis_size(axis_id), 2), 0),
+                axis_name=axis_id,
+                split_axis=0,
+                concat_axis=0,
+            ),
+            1,
+        )
+        return work_now
+
     factor_cols = factor.shape[1]
     per_device = factor.shape[0] // TILE
     tile_total = home.shape[0]
@@ -74,7 +87,7 @@
     ).astype(jnp.bfloat16)
     ladder = jnp.einsum(
         "iqa,bq->iab",
-        lax.all_to_all(back, "virt", split_axis=2, concat_axis=1, tiled=True),
+        points_obtain(back, "virt"),
         domain_coefficient,
         preferred_element_type=jnp.float32,
     )

time: 300 us -> 288 us (0.960)
  local copies, waits for them, and re-layouts: 54.1 us -> 44.4 us
    all_to_all x2 -> x0, local copies, waits for them, and re-layouts: 14.2 us -> none  [on_device(): lax.all_to_all(back, 'virt', split_axis=2, concat_axis=1, tiled=True)]
    unnamed x16 -> x27, local copies, waits for them, and re-layouts: 0.17 us -> 7.84 us
    convert_element_type x1 -> x0, local copies, waits for them, and re-layouts: 6.67 us -> none  [on_device(): back = jnp.einsum('iqp,ap->iqa', dressed, domain_coefficient, preferred_e...]
  transfers between devices with their start and end apart: 4 -> 4, of which waited for: 4 -> 4; matrix products, arithmetic and copies ran while one was open for 12% -> 13% of each run, Pallas kernels for 0% -> 0%
where the time goes in v1:
time: 288 us; the launch traced here: 287 us
  waiting for transfers between devices  95.6 us (33%)
  blocking collectives  51.6 us (18%)
  matrix products  45.4 us (16%)
  local copies, waits for them, and re-layouts  44.4 us (15%)
  other arithmetic  25.2 us (9%)
  between operations  14.3 us (5%)
  starting transfers between devices  10.6 us (4%)
    all_to_all x1, blocking collectives, on_device(): lax.all_to_all(half, 'virt', split_axis=1, concat_axis=2, tiled=True)  51.6 us
    ppermute x1, waiting for transfers between devices, with_halo(): after = lax.ppermute(first, axis, down)  42.6 us
    all_gather x1, waiting for transfers between devices, on_device(): arrived = lax.all_gather(outgoing, 'virt', axis=0, tiled=True)  39.4 us
    dot_general x1, matrix products, on_device(): jnp.einsum('iqa,bq->iab', points_obtain(back, 'virt'), domain_coefficient...  18.8 us
    mul x1, other arithmetic, on_device(): orbitals = domain_entry_row[spots // TILE] * TILE + spots % TILE  15.4 us
    dot_general x1, matrix products, on_device(): jnp.einsum('hjm,mf->hfj', cluster_amplitude, domain_coefficient, preferre...  12.6 us
    all_to_all x1, waiting for transfers between devices, points_obtain(): lax.all_to_all(jnp.stack(jnp.split(body, lax.axis_size(axis_id), 2), 0),...  12.3 us
    gather x1, local copies, waits for them, and re-layouts, on_device(): col_energy = virt_energy[orbitals]  11.8 us
  transfers between devices with their start and end apart: 4, of which 4 were waited for; matrix products, arithmetic and copies ran while one was open for 13% of the time, Pallas kernels for 0%

profile of v1, /device:TPU:0, one launch (start us, length us, event | category | flops | bytes accessed | tf_op | source)
XLA Modules:
  0.0 287.0 jit_solution(10474148213058548309)
XLA Ops:
  6.5 1.0 select_reduce_fusion
  8.7 0.9 broadcast_select_fusion
  9.7 39.4 %all-gather.2.cloned.1.call-done = bf16[32,64,1024]{2,1,0:T(8,128)(2,1)} async-done(((bf16[4,64,1024]{2,1,0:T(8,128)(2,1)}), bf16[32,64,1024]{2,1,0:T(8,128)(2,1)}) %all-gather.2.cloned.1.call-update) | async-done | bytes 4194320 | tf_op jit(solution)/shard_map/all_gather | solution.py:63
  49.1 5.0 %gather_fusion.1 = bf16[32,64,1024]{2,1,0:T(8,128)(2,1)} fusion(bf16[32,64,1024]{2,1,0:T(8,128)(2,1)} %all-gather.2.cloned.1.call-done, s32[1024]{0:T(1024)S(1)} %pad_clamp_fusion), kind=kCustom, calls=%fused_computation.1 | custom fusion | bytes 8388736 | tf_op jit(solution)/shard_map/gather | solution.py:64
  54.1 12.6 %convert_bitcast_fusion = bf16[8,1024,256]{2,1,0:T(8,128)(2,1)S(1)} fusion(bf16[2048,1024,1]{1,0,2:T(8,128)(2,1)} %bitcast.141, bf16[1,8,256,2048]{3,2,1,0:T(8,128)(2,1)} %param.9), kind=kOutput, calls=%fused_computation.15 | convolution fusion | flops 8592031744 | bytes 16777216 | tf_op jit(solution)/shard_map/hjm,mf->hfj/dot_general | solution.py:66
  66.7 2.4 copy.22
  69.2 51.6 %all_to_all.23 = bf16[8,1024,256]{2,0,1:T(8,128)(2,1)S(1)} all-to-all(bf16[8,1024,256]{2,0,1:T(8,128)(2,1)S(1)} %copy.22), channel_id=1, replica_groups=mesh['pair'=4,'virt'=8] {'virt'}, dimensions={1} | all-to-all | bytes 8388608 | tf_op jit(solution)/shard_map/all_to_all | solution.py:71
  120.7 4.3 %copy.30 = bf16[8,8,128,256]{3,1,2,0:T(8,128)(2,1)} copy(bf16[8,8,128,256]{3,0,2,1:T(8,128)(2,1)S(1)} %bitcast.139) | data formatting | bytes 8388608 | tf_op jit(solution)/shard_map/all_to_all | solution.py:71
  125.1 7.4 %all_to_all.19 = bf16[8,128,2048]{2,1,0:T(8,128)(2,1)} reshape(bf16[8,128,8,256]{3,2,1,0:T(8,128)(2,1)} %bitcast.140) | data formatting | bytes 8388608 | tf_op jit(solution)/shard_map/all_to_all | solution.py:71
  132.5 8.1 %convolution_convert_fusion.1 = bf16[8,128,1024]{2,1,0:T(8,128)(2,1)S(1)} fusion(bf16[8,128,2048]{2,1,0:T(8,128)(2,1)} %all_to_all.19, bf16[2048,1024,1]{1,0,2:T(8,128)(2,1)} %bitcast.142), kind=kOutput, calls=%fused_computation.23 | convolution fusion | flops 4296015872 | bytes 10485760 | tf_op jit(solution)/shard_map/iqd,dp->iqp/dot_general | solution.py:69
  140.6 1.3 collective-permute-start.1
  141.9 4.7 %collective-permute-start = (bf16[1,8,128,1024]{3,2,1,0:T(8,128)(2,1)S(1)}, bf16[1,8,128,1024]{3,2,1,0:T(8,128)(2,1)S(1)}, u32[]{:S(2)}, u32[]{:S(2)}) collective-permute-start(bf16[1,8,128,1024]{3,2,1,0:T(8,128)(2,1)S(1)} %bitcast.151), channel_id=1, source_target_pairs={{0,8},{8,16},{16,24},{1,9},{9,17},{17,25},{2,10},{10,18},{18,26},{... | collective-permute-start | bytes 6291464 | tf_op jit(solution)/shard_map/ppermute | solution.py:17
  146.7 42.6 %collective-permute-done.1 = bf16[1,8,128,1024]{3,2,1,0:T(8,128)(2,1)S(1)} collective-permute-done((bf16[1,8,128,1024]{3,2,1,0:T(8,128)(2,1)S(1)}, bf16[1,8,128,1024]{3,2,1,0:T(8,128)(2,1)S(1)}, u32[]{:S(2)}, u32[]{:S(2)}) %collective-permute-start.1) | collective-permute-done | bytes 2097184 | tf_op jit(solution)/shard_map/ppermute | solution.py:18
  189.3 1.2 collective-permute-done
  190.5 5.9 %convolution_convert_fusion = bf16[8,128,2048]{2,1,0:T(8,128)(2,1)S(1)} fusion(bf16[2048,1024,1]{1,0,2:T(8,128)(2,1)S(1)} %bitcast.143, bf16[8,128,1024]{2,1,0:T(8,128)(2,1)S(1)} %convolution_convert_fusion.1, bf16[1,8,128,1024]{3,2,1,0:T(8,128)(2,1)S(1)} %collective-permute-done.1, bf16[1,8,128,1024]{3,2,1,0:T(8,128)(2,1)S(1)} %collective-permute-done, ...), kind=kOutput, calls=%fused_computation.16 | convolution fusion | flops 4308598784 | bytes 15205888 | tf_op jit(solution)/shard_map/iqp,ap->iqa/dot_general | solution.py:85
  200.8 0.9 fusion.17
  203.5 4.7 %all-to-all-start.1 = ((bf16[8,8,128,256]{3,2,1,0:T(8,128)(2,1)}), bf16[8,8,128,256]{3,2,1,0:T(8,128)(2,1)}, u32[]{:S(2)}, u32[]{:S(2)}) async-start(bf16[8,8,128,256]{3,2,1,0:T(8,128)(2,1)} %fusion.15), calls=%async_computation.1 | async-start | bytes 8388608 | tf_op jit(solution)/shard_map/all_to_all | solution.py:27
  211.6 4.4 %compare_select_fusion.2 = s32[2048,1]{0,1:T(1,128)S(1)} fusion(s32[]{:T(128)} %bitcast.55, s32[]{:T(128)} %bitcast.56, s32[]{:T(128)} %bitcast.57, s32[]{:T(128)} %bitcast.58, s32[]{:T(128)} %bitcast.59, s32[]{:T(128)} %bitcast.61, s32[]{:T(128)} %bitcast.60), kind=kLoop, calls=%fused_computation.69 | loop fusion | flops 47104 | bytes 8220 | tf_op jit(solution)/shard_map/gather | solution.py:97
  216.0 15.4 %select_multiply_fusion = s32[2048]{0:T(1024)S(1)} fusion(pred[2048]{0:T(1024)(128)(4,1)S(1)} %compare_reduce_fusion, pred[2048]{0:T(1024)(128)(4,1)S(1)} %compare_reduce_fusion.1, pred[2048]{0:T(1024)(128)(4,1)S(1)} %compare_reduce_fusion.2, pred[2048]{0:T(1024)(128)(4,1)S(1)} %compare_reduce_fusion.3, pred[2048]{0:T(1024)(128)(4,1)S(1)} %compare_reduce_fusion.4, ...), kind=kLoop, calls=%fused_computation.85 | loop fusion | flops 53248 | bytes 67684 | tf_op jit(solution)/shard_map/mul | solution.py:97
  231.5 11.8 %gather_fusion.2 = f32[2048]{0:T(1024)S(1)} fusion(f32[8192]{0:T(1024)S(1)} %copy-done.2, s32[2048]{0:T(1024)S(1)} %broadcast_clamp_fusion), kind=kCustom, calls=%fused_computation.2 | custom fusion | bytes 24576 | tf_op jit(solution)/shard_map/gather | solution.py:98
  243.3 1.6 broadcast_add_fusion
  244.9 12.3 %all-to-all-done.1 = bf16[8,8,128,256]{3,2,1,0:T(8,128)(2,1)} async-done(((bf16[8,8,128,256]{3,2,1,0:T(8,128)(2,1)}), bf16[8,8,128,256]{3,2,1,0:T(8,128)(2,1)}, u32[]{:S(2)}, u32[]{:S(2)}) %all-to-all-start.1) | async-done | bytes 4194336 | tf_op jit(solution)/shard_map/all_to_all | solution.py:27
  257.3 2.6 copy.24
  261.4 18.8 %add_bitcast_fusion = f32[1,8,256,2048]{3,2,1,0:T(8,128)} fusion(bf16[1,8,256,2048]{3,2,1,0:T(8,128)(2,1)} %param.9, f32[]{:T(128)} %bitcast.137, f32[8]{0:T(128)S(1)} %copy-done.9, f32[256,2048]{1,0:T(8,128)S(1)} %copy-done.5, bf16[8,1024,256]{2,1,0:T(8,128)(2,1)S(1)} %bitcast.145, bf16[2048,1024,1]{1,0,2:T(8,128)(2,1)S(1)} %bitcast.144), kind=kOutput, calls=%fused_computation.3 | convolution fusion | flops 8610906112 | bytes 35651620 | tf_op jit(solution)/shard_map/iqa,bq->iab/dot_general | solution.py:88
  (72 shorter events, 11.9 us)
Async XLA Ops:
  6.5 1.6 copy-start
  6.5 42.6 %all-gather.2.cloned.1.call-start = ((), (), s32[]{:S(2)}) async-start(), calls=%async_computation.2 | async-start | bytes 4718592 | tf_op jit(solution)/shard_map/all_gather | solution.py:63
  132.5 14.1 %copy-start.8 = (bf16[1,3,128]{2,1,0:T(4,128)(2,1)S(1)}, bf16[1,3,128]{2,1,0:T(4,128)(2,1)}, u32[]{:S(2)}) copy-start(bf16[1,3,128]{2,1,0:T(4,128)(2,1)} %param.14) | copy-start | bytes 2308
  132.5 14.1 %copy-start.7 = (bf16[128,1024]{1,0:T(8,128)(2,1)S(1)}, bf16[128,1024]{1,0:T(8,128)(2,1)}, u32[]{:S(2)}) copy-start(bf16[128,1024]{1,0:T(8,128)(2,1)} %param.13) | copy-start | bytes 786436
  132.5 58.0 %copy-start.3 = (bf16[32,64,1024]{2,1,0:T(8,128)(2,1)S(1)}, bf16[32,64,1024]{2,1,0:T(8,128)(2,1)}, u32[]{:S(2)}) copy-start(bf16[32,64,1024]{2,1,0:T(8,128)(2,1)} %gather_fusion.1) | copy-start | bytes 12582916
  140.6 48.7 %collective-permute-start.1 = (bf16[1,8,128,1024]{3,2,1,0:T(8,128)(2,1)S(1)}, bf16[1,8,128,1024]{3,2,1,0:T(8,128)(2,1)S(1)}, u32[]{:S(2)}, u32[]{:S(2)}) collective-permute-start(bf16[1,8,128,1024]{3,2,1,0:T(8,128)(2,1)S(1)} %bitcast.150), channel_id=1, source_target_pairs={{8,0},{16,8},{24,16},{9,1},{17,9},{25,17},{10,2},{18,10},{26,18},{... | collective-permute-start | bytes 6291464 | tf_op jit(solution)/shard_map/ppermute | solution.py:18
  141.9 48.6 %collective-permute-start = (bf16[1,8,128,1024]{3,2,1,0:T(8,128)(2,1)S(1)}, bf16[1,8,128,1024]{3,2,1,0:T(8,128)(2,1)S(1)}, u32[]{:S(2)}, u32[]{:S(2)}) collective-permute-start(bf16[1,8,128,1024]{3,2,1,0:T(8,128)(2,1)S(1)} %bitcast.151), channel_id=1, source_target_pairs={{0,8},{8,16},{16,24},{1,9},{9,17},{17,25},{2,10},{10,18},{18,26},{... | collective-permute-start | bytes 6291464 | tf_op jit(solution)/shard_map/ppermute | solution.py:17
  203.5 6.7 %copy-start.6 = (s32[1,32]{1,0:T(1,128)S(1)}, s32[1,32]{1,0:T(1,128)}, u32[]{:S(2)}) copy-start(s32[1,32]{1,0:T(1,128)} %param.12) | copy-start | bytes 388
  203.5 28.0 %copy-start.2 = (f32[8192]{0:T(1024)S(1)}, f32[8192]{0:T(1024)}, u32[]{:S(2)}) copy-start(f32[8192]{0:T(1024)} %param.15) | copy-start | bytes 98308
  203.5 53.8 %all-to-all-start.1 = ((bf16[8,8,128,256]{3,2,1,0:T(8,128)(2,1)}), bf16[8,8,128,256]{3,2,1,0:T(8,128)(2,1)}, u32[]{:S(2)}, u32[]{:S(2)}) async-start(bf16[8,8,128,256]{3,2,1,0:T(8,128)(2,1)} %fusion.15), calls=%async_computation.1 | async-start | bytes 8388608 | tf_op jit(solution)/shard_map/all_to_all | solution.py:27
  257.2 3.4 %copy-start.4 = (bf16[32,64,1024]{2,1,0:T(8,128)(2,1)S(1)}, bf16[32,64,1024]{2,1,0:T(8,128)(2,1)}, u32[]{:S(2)}) copy-start(bf16[32,64,1024]{2,1,0:T(8,128)(2,1)} %gather_fusion.1) | copy-start | bytes 12582916
  257.2 4.1 %copy-start.5 = (f32[256,2048]{1,0:T(8,128)S(1)}, f32[256,2048]{1,0:T(8,128)}, u32[]{:S(2)}) copy-start(f32[256,2048]{1,0:T(8,128)} %broadcast_add_fusion) | copy-start | bytes 6291460
  257.3 4.1 %copy-start.9 = (f32[8]{0:T(128)S(1)}, f32[8]{0:T(128)}, u32[]{:S(2)}) copy-start(f32[8]{0:T(128)} %param.16) | copy-start | bytes 100
  261.4 18.8 %copy-start.1 = (bf16[1024,1024]{1,0:T(8,128)(2,1)S(1)}, bf16[1024,1024]{1,0:T(8,128)(2,1)}, u32[]{:S(2)}) copy-start(bf16[1024,1024]{1,0:T(8,128)(2,1)} %param.10) | copy-start | bytes 6291460
Sparse Core Ops, SparseCore 0:
  9.8 39.2 all-gather.1
